TPU v7x, 128 devices: a whole 4x4x4 slice. The times are simulated.
128 devices in a mesh: bead: 4 (over z_lo, core), space: 32 (over z_hi, x, y).
Axes of the slice: x: 4, y: 4, z: 4 (z_hi: 2, z_lo: 2; z = z_hi * 2 + z_lo), core: 2. Of those that a mesh axis runs over, the one named last changes fastest.
Arguments:
- centroid: float32 [3, 65536], P(None, 'space'), may hold values from 0 to 1
- bead_offsets: float32 [32, 3, 65536], P('bead', None, 'space'), may hold values from -0.6 to 0.6
- routes: int32 [65536, 1], P('space'), may hold values from 0 to 31; in each aligned block of 2048 rows (0 to 2047, 2048 to 4095, ...) at most 128 rows name the same one
Outputs:
- forces: float32 [32, 3, 65536], P('bead', None, 'space')
Inputs may be any that keep to these rules, and one draw needn't show every extreme that they name: `routes`: each molecule names one domain. The molecules of one slab name any one domain at most 128 times, a bound that some block reaches.
All inputs are finite; a program needn't handle non-finite values.
Results may differ from a plain program's by a relative error of at most 0.0003.
Values sent between devices are 32-bit elements; how exact they have to be, the bound alone decides.
No kernel may reach another device: no remote copies, remote signals or barrier semaphores. Data moves between devices by JAX's collectives and lax.ppermute only.
A program may use at most 64 MiB of HBM per device.

v0:
```python
import math

import jax
import jax.numpy as jnp
from jax import lax
from jax.sharding import PartitionSpec as P

BEADS = 32
CONTRACTED = 4


PAIR_SCALE = 0.1
BLOCK_ROWS = 512
REACH_SQUARED = 4.0
BODY_SCALE = 0.1
SLAB_SIDE = 1.5


def passed_along(value, axis, by):
    peers = lax.axis_size(axis)
    return lax.ppermute(value, axis, [(i, (i + by) % peers) for i in range(peers)])


def split_up(value, dim, peers):
    lengths = value.shape
    parts = value.reshape(*lengths[:dim], peers, lengths[dim] // peers, *lengths[dim + 1 :])
    return jnp.moveaxis(parts, dim, 0)


def summed_on_arrival(value, axis, dim):
    parts = split_up(value, dim, lax.axis_size(axis))
    arrived = lax.all_to_all(parts, axis, split_axis=0, concat_axis=0, tiled=True)
    return arrived.sum(axis=0)


def sent_to_all(value, axis):
    copies = jnp.broadcast_to(value, (lax.axis_size(axis), *value.shape))
    return lax.all_to_all(copies, axis, split_axis=0, concat_axis=0, tiled=True)


def laid_out(parts, dim):
    lengths = list(parts.shape[1:])
    lengths[dim] *= parts.shape[0]
    return jnp.moveaxis(parts, 0, dim).reshape(lengths)


def gathered_copies(value, axis, dim):
    parts = sent_to_all(value, axis)
    return laid_out(parts, dim)


def contract_table(beads, contracted):
    bead_pos = jnp.arange(beads).astype(jnp.float32)
    coarse = jnp.arange(contracted).astype(jnp.float32)
    phase = 2.0 * math.pi * (bead_pos[None, :] / beads - coarse[:, None] / contracted)
    return (1.0 + 2.0 * jnp.cos(phase)) / beads


def pair_terms(own, other):
    delta = own[:, :, None] - other[:, None, :]
    dist_sq = jnp.sum(delta * delta, axis=0)
    soft = jnp.maximum(1.0 - dist_sq, 0.0)
    weight = 6.0 * PAIR_SCALE * soft * soft
    pushed = weight[None] * delta
    return (jnp.sum(pushed, axis=2), -jnp.sum(pushed, axis=1))


def blocked_pairs(own, other):
    rows = own.shape[1]
    block = min(BLOCK_ROWS, rows)
    pieces = own.reshape(3, rows // block, block).transpose(1, 0, 2)

    def step(carry, piece):
        f_own, f_other = pair_terms(piece, other)
        return (carry + f_other, f_own)

    react, parts = lax.scan(step, jnp.zeros((3, other.shape[1]), jnp.float32), pieces)
    return (parts.transpose(1, 0, 2).reshape(3, rows), react)


def many_body(pos, valid):
    slots = pos.shape[1]
    block = min(BLOCK_ROWS, slots)
    count = slots // block
    pieces = pos.reshape(3, count, block).transpose(1, 0, 2)
    vpieces = valid.reshape(count, block)

    def weights(piece, vpiece):
        delta = piece[:, :, None] - pos[:, None, :]
        dist_sq = jnp.sum(delta * delta, axis=0)
        near = jnp.maximum(1.0 - dist_sq / REACH_SQUARED, 0.0)
        return (delta, vpiece[:, None] * valid[None, :] * near * near)

    density = lax.map(
        lambda item: jnp.sum(weights(item[0], item[1])[1], axis=1), (pieces, vpieces)
    ).reshape(slots)

    def force(item):
        piece, vpiece, rpiece = item
        delta, wgt = weights(piece, vpiece)
        coef = BODY_SCALE * (rpiece[:, None] + density[None, :]) * wgt * wgt
        return jnp.sum(coef[None] * delta, axis=2)

    parts = lax.map(force, (pieces, vpieces, density.reshape(count, block)))
    return parts.transpose(1, 0, 2).reshape(3, slots)


def shards(centroid, bead_offsets, routes):
    mol_dev = centroid.shape[1]
    beads_dev = bead_offsets.shape[0]
    domains = lax.axis_size("space")
    capacity = 2 * mol_dev // domains
    scale_vec = jnp.array([1.0, SLAB_SIDE, SLAB_SIDE], jnp.float32)
    unit_x = jnp.array([1.0, 0.0, 0.0], jnp.float32)
    q = scale_vec[None, :, None] * centroid[None] + bead_offsets
    nearby = passed_along(q, "space", -1) + unit_x[None, :, None]

    def one_bead(item):
        own, nxt = item
        inner, _ = blocked_pairs(own, own)
        cross, react = blocked_pairs(own, nxt)
        return (inner + cross, react)

    partial_pair, reaction = lax.map(one_bead, (q, nearby))
    pair2 = partial_pair + passed_along(reaction, "space", 1)
    contract = contract_table(BEADS, CONTRACTED)
    first = lax.axis_index("bead") * beads_dev
    local_contract = lax.dynamic_slice_in_dim(contract, first, beads_dev, 1)
    partial_value = jnp.einsum("kb,bcm->kcm", local_contract, q, precision=lax.Precision.HIGHEST)
    coarse_pos = summed_on_arrival(partial_value, "bead", 0)
    slab = lax.axis_index("space").astype(jnp.float32)
    coarse_pos = coarse_pos + unit_x[None, :, None] * slab
    coarse_dev = coarse_pos.shape[0]
    route = routes[:, 0]
    onehot = (route[:, None] == jnp.arange(domains)[None, :]).astype(jnp.int32)
    ranks = jnp.cumsum(onehot, axis=0)
    slot = jnp.sum(onehot * ranks, axis=1) - 1
    stacked = jnp.concatenate([coarse_pos, jnp.ones((coarse_dev, 1, mol_dev), jnp.float32)], axis=1)
    outbox = (
        jnp.zeros((coarse_dev, 4, domains, capacity), jnp.float32)
        .at[:, :, route, slot]
        .set(stacked)
    )
    inbox = lax.all_to_all(outbox, "space", split_axis=2, concat_axis=2, tiled=True)
    flat = inbox.reshape(coarse_dev, 4, domains * capacity)
    domain_force = lax.map(lambda item: many_body(item[:3], item[3]) * item[3][None, :], flat)
    returned = lax.all_to_all(
        domain_force.reshape(coarse_dev, 3, domains, capacity),
        "space",
        split_axis=2,
        concat_axis=2,
        tiled=True,
    )
    mine = returned[:, :, route, slot]
    every_coarse = gathered_copies(mine, "bead", 0)
    expand = lax.dynamic_slice_in_dim(contract, first, beads_dev, 1).T * (BEADS / CONTRACTED)
    spread = jnp.einsum("bk,kcm->bcm", expand, every_coarse, precision=lax.Precision.HIGHEST)
    return pair2 + spread


def solution(mesh):
    placed = (P(None, "space"), P("bead", None, "space"), P("space", None))
    return jax.shard_map(
        shards, mesh=mesh, in_specs=placed, out_specs=P("bead", None, "space"), check_vma=False
    )
```

profile of v0, /device:TPU:1, one launch (start us, length us, event | category | flops | bytes accessed | tf_op | source)
XLA Modules:
  0.0 537.0 jit_solution(3608041790922502651)
XLA Ops:
  9.2 9.1 %reduce-window.6 = s32[32,16,128]{2,1,0:T(8,128)S(1)} reduce-window(s32[32,16,128]{2,1,0:T(8,128)S(1)} %fusion.12, s32[]{:T(128)} %constant.96.clone.1), window={size=1x1x128 pad=0_0x0_0x127_0}, to_apply=%region_11.12 | reduce-window | flops 8323072 | bytes 524292 | tf_op jit(solution)/shard_map/reduce-window
  30.6 10.4 %all-to-all-start.1 = ((f32[1,4,32,128]{3,1,0,2:T(4,128)}), f32[1,4,32,128]{3,1,0,2:T(4,128)S(1)}, u32[]{:S(2)}, u32[]{:S(2)}) async-start(f32[1,4,32,128]{3,1,0,2:T(4,128)} %copy.88), calls=%async_computation.1 | async-start | bytes 131072 | tf_op jit(solution)/shard_map/all_to_all | solution.py:144
  41.1 7.1 %collective-permute-start = (f32[8,3,2048]{2,1,0:T(4,128)S(1)}, f32[8,3,2048]{2,1,0:T(4,128)}, u32[]{:S(2)}, u32[]{:S(2)}) collective-permute-start(f32[8,3,2048]{2,1,0:T(4,128)S(1)} %copy_add_fusion), channel_id=1, source_target_pairs={{0,31},{1,0},{2,1},{3,2},{4,3},{5,4},{6,5},{7,6},{8,7},{9,8},{10,9... | collective-permute-start | bytes 589832 | tf_op jit(solution)/shard_map/ppermute | solution.py:21
  49.9 44.9 %while.68 = (s32[]{:T(128)}, f32[8,512]{1,0:T(8,128)S(1)}, f32[8,512]{1,0:T(8,128)S(1)}, f32[1,4096]{1,0:T(1,128)S(1)}, f32[8,3,512]{2,1,0:T(4,128)S(1)}, /*index=5*/f32[3,4096]{1,0:T(4,128)S(1)}, s32[]{:T(128)}, s32[]{:T(128)}) while((s32[]{:T(128)}, f32[8,512]{1,0:T(8,128)S(1)}, f32[8,512]{1,0:T(8,128)S(1)}, f32[1,4096]{1,0:T(1,128)S(1)}, ...), condition=%wide.region_19.20_spmd, body=%wide.region_16.19_spmd.sunk | while | flops 31456768 | bytes 16873568 | solution.py:94
  94.9 116.6 %while.69 = (s32[]{:T(128)}, f32[8,3,512]{2,1,0:T(4,128)S(1)}, f32[8,512]{1,0:T(8,128)S(1)}, f32[8,512]{1,0:T(8,128)S(1)}, f32[1,4096]{1,0:T(1,128)S(1)}, /*inde...) while((s32[]{:T(128)}, f32[8,3,512]{2,1,0:T(4,128)S(1)}, f32[8,512]{1,0:T(8,128)S(1)}, ...), condition=%wide.region_23.24_spmd, body=%wide.region_20.23_spmd.sunk | while | flops 56621568 | bytes 33777760 | solution.py:104
  103.3 6.2 %fusion.38 = f32[3,512]{1,0:T(4,128)S(1)} fusion(f32[512,4096]{1,0:T(8,128)} %multiply_multiply_fusion.8, f32[3,4096]{1,0:T(4,128)S(1)} %get-tuple-element.597, f32[3,512]{1,0:T(4,128)S(1)} %dynamic-slice_bitcast_fusion.12), kind=kLoop, calls=%fused_computation.17.clone.1 | loop fusion | flops 18872832 | bytes 8450048 | tf_op jit(solution)/shard_map/while/body/eval_jaxpr/while/body/eval_jaxpr/reduce_sum | solution.py:102
  117.9 6.2 %fusion.38 = f32[3,512]{1,0:T(4,128)S(1)} fusion(f32[512,4096]{1,0:T(8,128)} %multiply_multiply_fusion.8, f32[3,4096]{1,0:T(4,128)S(1)} %get-tuple-element.597, f32[3,512]{1,0:T(4,128)S(1)} %dynamic-slice_bitcast_fusion.12), kind=kLoop, calls=%fused_computation.17.clone.1 | loop fusion | flops 18872832 | bytes 8450048 | tf_op jit(solution)/shard_map/while/body/eval_jaxpr/while/body/eval_jaxpr/reduce_sum | solution.py:102
  132.4 6.2 %fusion.38 = f32[3,512]{1,0:T(4,128)S(1)} fusion(f32[512,4096]{1,0:T(8,128)} %multiply_multiply_fusion.8, f32[3,4096]{1,0:T(4,128)S(1)} %get-tuple-element.597, f32[3,512]{1,0:T(4,128)S(1)} %dynamic-slice_bitcast_fusion.12), kind=kLoop, calls=%fused_computation.17.clone.1 | loop fusion | flops 18872832 | bytes 8450048 | tf_op jit(solution)/shard_map/while/body/eval_jaxpr/while/body/eval_jaxpr/reduce_sum | solution.py:102
  147.0 6.2 %fusion.38 = f32[3,512]{1,0:T(4,128)S(1)} fusion(f32[512,4096]{1,0:T(8,128)} %multiply_multiply_fusion.8, f32[3,4096]{1,0:T(4,128)S(1)} %get-tuple-element.597, f32[3,512]{1,0:T(4,128)S(1)} %dynamic-slice_bitcast_fusion.12), kind=kLoop, calls=%fused_computation.17.clone.1 | loop fusion | flops 18872832 | bytes 8450048 | tf_op jit(solution)/shard_map/while/body/eval_jaxpr/while/body/eval_jaxpr/reduce_sum | solution.py:102
  161.5 6.2 %fusion.38 = f32[3,512]{1,0:T(4,128)S(1)} fusion(f32[512,4096]{1,0:T(8,128)} %multiply_multiply_fusion.8, f32[3,4096]{1,0:T(4,128)S(1)} %get-tuple-element.597, f32[3,512]{1,0:T(4,128)S(1)} %dynamic-slice_bitcast_fusion.12), kind=kLoop, calls=%fused_computation.17.clone.1 | loop fusion | flops 18872832 | bytes 8450048 | tf_op jit(solution)/shard_map/while/body/eval_jaxpr/while/body/eval_jaxpr/reduce_sum | solution.py:102
  176.1 6.2 %fusion.38 = f32[3,512]{1,0:T(4,128)S(1)} fusion(f32[512,4096]{1,0:T(8,128)} %multiply_multiply_fusion.8, f32[3,4096]{1,0:T(4,128)S(1)} %get-tuple-element.597, f32[3,512]{1,0:T(4,128)S(1)} %dynamic-slice_bitcast_fusion.12), kind=kLoop, calls=%fused_computation.17.clone.1 | loop fusion | flops 18872832 | bytes 8450048 | tf_op jit(solution)/shard_map/while/body/eval_jaxpr/while/body/eval_jaxpr/reduce_sum | solution.py:102
  216.0 8.7 %all-to-all-done.2 = f32[1,3,32,128]{3,0,1,2:T(1,128)S(1)} async-done(((f32[1,3,32,128]{3,0,1,2:T(1,128)}), f32[1,3,32,128]{3,0,1,2:T(1,128)S(1)}, u32[]{:S(2)}, u32[]{:S(2)}) %all-to-all-start.2) | async-done | bytes 49184 | tf_op jit(solution)/shard_map/all_to_all | solution.py:147
  225.4 13.0 %gather_fusion = f32[2048,3]{1,0:T(8,128)S(1)} fusion(f32[3,32,128]{0,2,1:T(8,128)S(1)} %bitcast.133, s32[2048]{0:T(1024)S(1)} %bitcast.128), kind=kCustom, calls=%fused_computation | custom fusion | bytes 65536 | tf_op jit(solution)/shard_map/gather | solution.py:154
  239.4 6.5 %all-to-all-start.3 = ((f32[4,1,3,2048]{3,1,2,0:T(1,128)}), f32[4,1,3,2048]{3,1,2,0:T(1,128)}, u32[]{:S(2)}, u32[]{:S(2)}) async-start(f32[4,1,3,2048]{3,1,2,0:T(1,128)} %broadcast_in_dim.31), calls=%async_computation.3 | async-start | bytes 196608 | tf_op jit(solution)/shard_map/all_to_all | solution.py:38
  247.0 276.3 %while.67 = (s32[]{:T(128)}, f32[8,3,2048]{2,0,1:T(8,128)}, f32[8,3,2048]{2,0,1:T(8,128)}, f32[8,3,2048]{2,1,0:T(4,128)S(1)}, f32[8,3,2048]{2,1,0:T(4,128)S(1)},...) while((s32[]{:T(128)}, f32[8,3,2048]{2,0,1:T(8,128)}, ...), condition=%wide.region_10.11_spmd, body=%wide.region_0.10_spmd.sunk | while | flops 47201280 | bytes 34312600 | solution.py:124
  247.1 17.3 %while.71 = (s32[]{:T(128)}, f32[3,2048]{1,0:T(4,128)S(1)}, f32[4,3,512]{2,1,0:T(4,128)S(1)}, f32[4,3,512]{2,1,0:T(4,128)S(1)}, f32[3,2048]{1,0:T(4,128)S(1)}, /*index=5*/s32[]{:T(128)}, s32[]{:T(128)}) while((s32[]{:T(128)}, f32[3,2048]{1,0:T(4,128)S(1)}, f32[4,3,512]{2,1,0:T(4,128)S(1)}, f32[4,3,512]{2,1,0:T(4,128)S(1)}, ...), condition=%wide.region_9.9_spmd.clone, body=%wide.region_5.8_spmd.clone.sunk | while | flops 25176576 | bytes 16971868 | solution.py:77
  264.5 13.7 %while.70 = (s32[]{:T(128)}, f32[4,3,512]{2,1,0:T(4,128)S(1)}, f32[4,3,512]{2,1,0:T(4,128)S(1)}, f32[3,2048]{1,0:T(4,128)S(1)}, s32[]{:T(128)}) while((s32[]{:T(128)}, f32[4,3,512]{2,1,0:T(4,128)S(1)}, f32[4,3,512]{2,1,0:T(4,128)S(1)}, f32[3,2048]{1,0:T(4,128)S(1)}, s32[]{:T(128)}) %tuple.120), condition=%wide.region_4.4_spmd, body=%wide.region_1.3_spmd.sunk | while | flops 22018560 | bytes 16873540 | solution.py:77
  281.6 17.3 %while.71 = (s32[]{:T(128)}, f32[3,2048]{1,0:T(4,128)S(1)}, f32[4,3,512]{2,1,0:T(4,128)S(1)}, f32[4,3,512]{2,1,0:T(4,128)S(1)}, f32[3,2048]{1,0:T(4,128)S(1)}, /*index=5*/s32[]{:T(128)}, s32[]{:T(128)}) while((s32[]{:T(128)}, f32[3,2048]{1,0:T(4,128)S(1)}, f32[4,3,512]{2,1,0:T(4,128)S(1)}, f32[4,3,512]{2,1,0:T(4,128)S(1)}, ...), condition=%wide.region_9.9_spmd.clone, body=%wide.region_5.8_spmd.clone.sunk | while | flops 25176576 | bytes 16971868 | solution.py:77
  299.0 13.7 %while.70 = (s32[]{:T(128)}, f32[4,3,512]{2,1,0:T(4,128)S(1)}, f32[4,3,512]{2,1,0:T(4,128)S(1)}, f32[3,2048]{1,0:T(4,128)S(1)}, s32[]{:T(128)}) while((s32[]{:T(128)}, f32[4,3,512]{2,1,0:T(4,128)S(1)}, f32[4,3,512]{2,1,0:T(4,128)S(1)}, f32[3,2048]{1,0:T(4,128)S(1)}, s32[]{:T(128)}) %tuple.120), condition=%wide.region_4.4_spmd, body=%wide.region_1.3_spmd.sunk | while | flops 22018560 | bytes 16873540 | solution.py:77
  316.2 17.3 %while.71 = (s32[]{:T(128)}, f32[3,2048]{1,0:T(4,128)S(1)}, f32[4,3,512]{2,1,0:T(4,128)S(1)}, f32[4,3,512]{2,1,0:T(4,128)S(1)}, f32[3,2048]{1,0:T(4,128)S(1)}, /*index=5*/s32[]{:T(128)}, s32[]{:T(128)}) while((s32[]{:T(128)}, f32[3,2048]{1,0:T(4,128)S(1)}, f32[4,3,512]{2,1,0:T(4,128)S(1)}, f32[4,3,512]{2,1,0:T(4,128)S(1)}, ...), condition=%wide.region_9.9_spmd.clone, body=%wide.region_5.8_spmd.clone.sunk | while | flops 25176576 | bytes 16971868 | solution.py:77
  333.5 13.7 %while.70 = (s32[]{:T(128)}, f32[4,3,512]{2,1,0:T(4,128)S(1)}, f32[4,3,512]{2,1,0:T(4,128)S(1)}, f32[3,2048]{1,0:T(4,128)S(1)}, s32[]{:T(128)}) while((s32[]{:T(128)}, f32[4,3,512]{2,1,0:T(4,128)S(1)}, f32[4,3,512]{2,1,0:T(4,128)S(1)}, f32[3,2048]{1,0:T(4,128)S(1)}, s32[]{:T(128)}) %tuple.120), condition=%wide.region_4.4_spmd, body=%wide.region_1.3_spmd.sunk | while | flops 22018560 | bytes 16873540 | solution.py:77
  350.7 17.3 %while.71 = (s32[]{:T(128)}, f32[3,2048]{1,0:T(4,128)S(1)}, f32[4,3,512]{2,1,0:T(4,128)S(1)}, f32[4,3,512]{2,1,0:T(4,128)S(1)}, f32[3,2048]{1,0:T(4,128)S(1)}, /*index=5*/s32[]{:T(128)}, s32[]{:T(128)}) while((s32[]{:T(128)}, f32[3,2048]{1,0:T(4,128)S(1)}, f32[4,3,512]{2,1,0:T(4,128)S(1)}, f32[4,3,512]{2,1,0:T(4,128)S(1)}, ...), condition=%wide.region_9.9_spmd.clone, body=%wide.region_5.8_spmd.clone.sunk | while | flops 25176576 | bytes 16971868 | solution.py:77
  368.1 13.7 %while.70 = (s32[]{:T(128)}, f32[4,3,512]{2,1,0:T(4,128)S(1)}, f32[4,3,512]{2,1,0:T(4,128)S(1)}, f32[3,2048]{1,0:T(4,128)S(1)}, s32[]{:T(128)}) while((s32[]{:T(128)}, f32[4,3,512]{2,1,0:T(4,128)S(1)}, f32[4,3,512]{2,1,0:T(4,128)S(1)}, f32[3,2048]{1,0:T(4,128)S(1)}, s32[]{:T(128)}) %tuple.120), condition=%wide.region_4.4_spmd, body=%wide.region_1.3_spmd.sunk | while | flops 22018560 | bytes 16873540 | solution.py:77
  385.2 17.3 %while.71 = (s32[]{:T(128)}, f32[3,2048]{1,0:T(4,128)S(1)}, f32[4,3,512]{2,1,0:T(4,128)S(1)}, f32[4,3,512]{2,1,0:T(4,128)S(1)}, f32[3,2048]{1,0:T(4,128)S(1)}, /*index=5*/s32[]{:T(128)}, s32[]{:T(128)}) while((s32[]{:T(128)}, f32[3,2048]{1,0:T(4,128)S(1)}, f32[4,3,512]{2,1,0:T(4,128)S(1)}, f32[4,3,512]{2,1,0:T(4,128)S(1)}, ...), condition=%wide.region_9.9_spmd.clone, body=%wide.region_5.8_spmd.clone.sunk | while | flops 25176576 | bytes 16971868 | solution.py:77
  402.6 13.7 %while.70 = (s32[]{:T(128)}, f32[4,3,512]{2,1,0:T(4,128)S(1)}, f32[4,3,512]{2,1,0:T(4,128)S(1)}, f32[3,2048]{1,0:T(4,128)S(1)}, s32[]{:T(128)}) while((s32[]{:T(128)}, f32[4,3,512]{2,1,0:T(4,128)S(1)}, f32[4,3,512]{2,1,0:T(4,128)S(1)}, f32[3,2048]{1,0:T(4,128)S(1)}, s32[]{:T(128)}) %tuple.120), condition=%wide.region_4.4_spmd, body=%wide.region_1.3_spmd.sunk | while | flops 22018560 | bytes 16873540 | solution.py:77
  419.7 17.3 %while.71 = (s32[]{:T(128)}, f32[3,2048]{1,0:T(4,128)S(1)}, f32[4,3,512]{2,1,0:T(4,128)S(1)}, f32[4,3,512]{2,1,0:T(4,128)S(1)}, f32[3,2048]{1,0:T(4,128)S(1)}, /*index=5*/s32[]{:T(128)}, s32[]{:T(128)}) while((s32[]{:T(128)}, f32[3,2048]{1,0:T(4,128)S(1)}, f32[4,3,512]{2,1,0:T(4,128)S(1)}, f32[4,3,512]{2,1,0:T(4,128)S(1)}, ...), condition=%wide.region_9.9_spmd.clone, body=%wide.region_5.8_spmd.clone.sunk | while | flops 25176576 | bytes 16971868 | solution.py:77
  437.1 13.7 %while.70 = (s32[]{:T(128)}, f32[4,3,512]{2,1,0:T(4,128)S(1)}, f32[4,3,512]{2,1,0:T(4,128)S(1)}, f32[3,2048]{1,0:T(4,128)S(1)}, s32[]{:T(128)}) while((s32[]{:T(128)}, f32[4,3,512]{2,1,0:T(4,128)S(1)}, f32[4,3,512]{2,1,0:T(4,128)S(1)}, f32[3,2048]{1,0:T(4,128)S(1)}, s32[]{:T(128)}) %tuple.120), condition=%wide.region_4.4_spmd, body=%wide.region_1.3_spmd.sunk | while | flops 22018560 | bytes 16873540 | solution.py:77
  454.3 17.3 %while.71 = (s32[]{:T(128)}, f32[3,2048]{1,0:T(4,128)S(1)}, f32[4,3,512]{2,1,0:T(4,128)S(1)}, f32[4,3,512]{2,1,0:T(4,128)S(1)}, f32[3,2048]{1,0:T(4,128)S(1)}, /*index=5*/s32[]{:T(128)}, s32[]{:T(128)}) while((s32[]{:T(128)}, f32[3,2048]{1,0:T(4,128)S(1)}, f32[4,3,512]{2,1,0:T(4,128)S(1)}, f32[4,3,512]{2,1,0:T(4,128)S(1)}, ...), condition=%wide.region_9.9_spmd.clone, body=%wide.region_5.8_spmd.clone.sunk | while | flops 25176576 | bytes 16971868 | solution.py:77
  471.6 13.7 %while.70 = (s32[]{:T(128)}, f32[4,3,512]{2,1,0:T(4,128)S(1)}, f32[4,3,512]{2,1,0:T(4,128)S(1)}, f32[3,2048]{1,0:T(4,128)S(1)}, s32[]{:T(128)}) while((s32[]{:T(128)}, f32[4,3,512]{2,1,0:T(4,128)S(1)}, f32[4,3,512]{2,1,0:T(4,128)S(1)}, f32[3,2048]{1,0:T(4,128)S(1)}, s32[]{:T(128)}) %tuple.120), condition=%wide.region_4.4_spmd, body=%wide.region_1.3_spmd.sunk | while | flops 22018560 | bytes 16873540 | solution.py:77
  488.8 17.3 %while.71 = (s32[]{:T(128)}, f32[3,2048]{1,0:T(4,128)S(1)}, f32[4,3,512]{2,1,0:T(4,128)S(1)}, f32[4,3,512]{2,1,0:T(4,128)S(1)}, f32[3,2048]{1,0:T(4,128)S(1)}, /*index=5*/s32[]{:T(128)}, s32[]{:T(128)}) while((s32[]{:T(128)}, f32[3,2048]{1,0:T(4,128)S(1)}, f32[4,3,512]{2,1,0:T(4,128)S(1)}, f32[4,3,512]{2,1,0:T(4,128)S(1)}, ...), condition=%wide.region_9.9_spmd.clone, body=%wide.region_5.8_spmd.clone.sunk | while | flops 25176576 | bytes 16971868 | solution.py:77
  506.2 13.7 %while.70 = (s32[]{:T(128)}, f32[4,3,512]{2,1,0:T(4,128)S(1)}, f32[4,3,512]{2,1,0:T(4,128)S(1)}, f32[3,2048]{1,0:T(4,128)S(1)}, s32[]{:T(128)}) while((s32[]{:T(128)}, f32[4,3,512]{2,1,0:T(4,128)S(1)}, f32[4,3,512]{2,1,0:T(4,128)S(1)}, f32[3,2048]{1,0:T(4,128)S(1)}, s32[]{:T(128)}) %tuple.120), condition=%wide.region_4.4_spmd, body=%wide.region_1.3_spmd.sunk | while | flops 22018560 | bytes 16873540 | solution.py:77
  524.9 10.5 %collective-permute-done.1 = f32[8,3,2048]{2,0,1:T(8,128)S(1)} collective-permute-done((f32[8,3,2048]{2,0,1:T(8,128)}, f32[8,3,2048]{2,0,1:T(8,128)S(1)}, u32[]{:S(2)}, u32[]{:S(2)}) %collective-permute-start.1) | collective-permute-done | bytes 196640 | tf_op jit(solution)/shard_map/ppermute | solution.py:21
  (588 shorter events, 429.5 us)
Async XLA Ops:
  2.0 0.6 copy-start
  3.8 18.9 %all-to-all-start = ((f32[4,1,3,2048]{3,1,2,0:T(1,128)}), f32[4,1,3,2048]{3,1,2,0:T(1,128)S(1)}, u32[]{:S(2)}, u32[]{:S(2)}) async-start(f32[4,1,3,2048]{3,1,2,0:T(1,128)} %copy.85), calls=%async_computation | async-start | bytes 196608 | tf_op jit(solution)/shard_map/all_to_all | solution.py:32
  30.6 19.2 %all-to-all-start.1 = ((f32[1,4,32,128]{3,1,0,2:T(4,128)}), f32[1,4,32,128]{3,1,0,2:T(4,128)S(1)}, u32[]{:S(2)}, u32[]{:S(2)}) async-start(f32[1,4,32,128]{3,1,0,2:T(4,128)} %copy.88), calls=%async_computation.1 | async-start | bytes 131072 | tf_op jit(solution)/shard_map/all_to_all | solution.py:144
  41.1 204.9 %collective-permute-start = (f32[8,3,2048]{2,1,0:T(4,128)S(1)}, f32[8,3,2048]{2,1,0:T(4,128)}, u32[]{:S(2)}, u32[]{:S(2)}) collective-permute-start(f32[8,3,2048]{2,1,0:T(4,128)S(1)} %copy_add_fusion), channel_id=1, source_target_pairs={{0,31},{1,0},{2,1},{3,2},{4,3},{5,4},{6,5},{7,6},{8,7},{9,8},{10,9... | collective-permute-start | bytes 589832 | tf_op jit(solution)/shard_map/ppermute | solution.py:21
  94.9 151.1 %copy-start.2 = (f32[3]{0:T(128)S(1)}, f32[3]{0:T(128)}, u32[]{:S(2)}) copy-start(f32[3]{0:T(128)} %constant.150.clone) | copy-start | bytes 40
  212.2 12.5 %all-to-all-start.2 = ((f32[1,3,32,128]{3,0,1,2:T(1,128)}), f32[1,3,32,128]{3,0,1,2:T(1,128)S(1)}, u32[]{:S(2)}, u32[]{:S(2)}) async-start(f32[1,3,32,128]{3,0,1,2:T(1,128)} %copy.94), calls=%async_computation.2 | async-start | bytes 98304 | tf_op jit(solution)/shard_map/all_to_all | solution.py:147
  239.4 284.1 %all-to-all-start.3 = ((f32[4,1,3,2048]{3,1,2,0:T(1,128)}), f32[4,1,3,2048]{3,1,2,0:T(1,128)}, u32[]{:S(2)}, u32[]{:S(2)}) async-start(f32[4,1,3,2048]{3,1,2,0:T(1,128)} %broadcast_in_dim.31), calls=%async_computation.3 | async-start | bytes 196608 | tf_op jit(solution)/shard_map/all_to_all | solution.py:38
  247.0 276.6 %copy-start.1 = (f32[4,32]{1,0:T(4,128)S(1)}, f32[4,32]{1,0:T(4,128)}, u32[]{:S(2)}) copy-start(f32[4,32]{1,0:T(4,128)} %copy-done) | copy-start | bytes 1540
  523.3 12.1 %collective-permute-start.1 = (f32[8,3,2048]{2,0,1:T(8,128)}, f32[8,3,2048]{2,0,1:T(8,128)S(1)}, u32[]{:S(2)}, u32[]{:S(2)}) collective-permute-start(f32[8,3,2048]{2,0,1:T(8,128)} %get-tuple-element.162), channel_id=1, source_target_pairs={{0,1},{1,2},{2,3},{3,4},{4,5},{5,6},{6,7},{7,8},{8,9},{9,10},{10,1... | collective-permute-start | bytes 589832 | tf_op jit(solution)/shard_map/ppermute | solution.py:21
where the time goes:
time: 538 us; the launch traced here: 537 us
  other arithmetic  422 us (78%)
  local copies, waits for them, and re-layouts  54.8 us (10%)
  starting transfers between devices  32.9 us (6%)
  waiting for transfers between devices  20.7 us (4%)
    reduce_sum x64, other arithmetic, pair_terms(): return (jnp.sum(pushed, axis=2), -jnp.sum(pushed, axis=1))  122 us
    reduce_sum x64, other arithmetic, pair_terms(): dist_sq = jnp.sum(delta * delta, axis=0)  79.1 us
    reduce_sum x16, other arithmetic, weights(): dist_sq = jnp.sum(delta * delta, axis=0)  51 us
    reduce_sum x8, other arithmetic, force(): return jnp.sum(coef[None] * delta, axis=2)  50 us
    mul x64, other arithmetic, pair_terms(): weight = 6.0 * PAIR_SCALE * soft * soft  42.2 us
    mul x8, other arithmetic, force(): coef = BODY_SCALE * (rpiece[:, None] + density[None, :]) * wgt * wgt  40.2 us
    dynamic_update_slice x32, local copies, waits for them, and re-layouts, shards(): partial_pair, reaction = lax.map(one_bead, (q, nearby))  27.4 us
    reduce_sum x8, other arithmetic, many_body(): jnp.sum(weights(item[0], item[1])[1], axis=1)  18.4 us
  transfers between devices with their start and end apart: 6, of which 3 were waited for; matrix products, arithmetic and copies ran while one was open for 87% of the time, Pallas kernels for 0%

commit v1 on v0

v1 whole, which is shorter than its diff:
```python
import functools
import math

import jax
import jax.numpy as jnp
import numpy as np
from jax import lax
from jax.experimental import pallas as pl
from jax.experimental.pallas import tpu as pltpu
from jax.sharding import PartitionSpec as P

BEADS = 32
CONTRACTED = 4
PAIR_SCALE = 0.1
BODY_SCALE = 0.1
SLAB_SIDE = 1.5
BAND = 4
FAR = 64.0

f32, bf16 = jnp.float32, jnp.bfloat16
VMEM = pltpu.VMEM


def contract_table():
    phase = 2.0 * math.pi * (np.arange(BEADS)[None, :] / BEADS - np.arange(CONTRACTED)[:, None] / CONTRACTED)
    return ((1.0 + 2.0 * np.cos(phase)) / BEADS).astype(np.float32)


def passed_along(value, axis, by):
    peers = lax.axis_size(axis)
    return lax.ppermute(value, axis, [(i, (i + by) % peers) for i in range(peers)])


def thirds(x):
    high = x.astype(bf16).astype(f32)
    rest = x - high
    mid = rest.astype(bf16).astype(f32)
    return high, mid, rest - mid


def factors(p, reach_sq):
    unit = 1.0 / reach_sq
    high, mid, low = thirds(p)
    norm = 0.5 - unit * jnp.sum(p * p, axis=0, keepdims=True)
    nh, nm, nl = thirds(norm)
    one = jnp.ones_like(norm)
    two = 2.0 * unit
    pad = jnp.zeros((2, p.shape[1]), f32)
    left = [two * high, two * high, two * mid, two * mid, two * high, two * low, two * mid, two * low]
    right = [high, mid, high, mid, low, high, low, mid]
    left = jnp.concatenate(left + [nh, nm, nl, one, one, one, pad], axis=0)
    right = jnp.concatenate(right + [one, one, one, nh, nm, nl, pad], axis=0)
    return left, right


def centre(shift):
    row = lax.broadcasted_iota(jnp.int32, (3, 1), 0)
    return jnp.where(row == 0, 0.5 + shift, 0.5 * SLAB_SIDE).astype(f32)


PAIR_ROWS = 256
PAIR_LANES = 1024


def pair_kernel(shifts, adds, *refs):
    own_ref = refs[0]
    other_refs = refs[1 : 1 + len(shifts)]
    base_ref = refs[1 + len(shifts)] if adds else None
    out_ref, left_s, right_s, terms_s, weight_s, acc_s = refs[-6:]
    mols = own_ref.shape[-1]
    own = own_ref[0] - centre(0.0)
    _, right = factors(own, 1.0)
    right_s[...] = right.astype(bf16)
    acc_s[...] = jnp.zeros_like(acc_s)
    rows = PAIR_ROWS
    steps = mols // rows
    for ref, shift in zip(other_refs, shifts):
        other = ref[0] - centre(-shift)
        left, _ = factors(other, 1.0)
        left_s[...] = left.T.astype(bf16)
        one = jnp.ones((1, mols), f32)
        terms_s[...] = jnp.concatenate([one, *thirds(other), jnp.zeros((6, mols), f32)], axis=0).astype(bf16)

        def weigh(step, slot):
            at = pl.ds(pl.multiple_of(step * rows, rows), rows)
            for lo in range(0, mols, PAIR_LANES):
                lanes = slice(lo, lo + PAIR_LANES)
                soft = jnp.dot(left_s[at, :], right_s[:, lanes], preferred_element_type=f32)
                soft = jnp.maximum(soft, 0.0)
                weight_s[slot, :, lanes] = (soft * soft).astype(bf16)

        def push(step, slot):
            at = pl.ds(pl.multiple_of(step * rows, rows), rows)
            acc_s[...] += jnp.dot(terms_s[:, at], weight_s[slot], preferred_element_type=f32)

        weigh(0, 0)

        def two_steps(turn, carry):
            step = 2 * turn
            weigh(step + 1, 1)
            push(step, 0)
            weigh(jnp.minimum(step + 2, steps - 1), 0)
            push(step + 1, 1)
            return carry

        lax.fori_loop(0, steps // 2, two_steps, 0)
    total = acc_s[...]
    moved = total[1:4] + total[4:7] + total[7:10]
    force = (own * total[0:1] - moved) * f32(6.0 * PAIR_SCALE)
    out_ref[0] = force + base_ref[0] if adds else force


def pair_forces(own, others, shifts, base, first, count):
    mols = own.shape[-1]
    block = pl.BlockSpec((1, 3, mols), lambda b: (b + first if first else b, 0, 0))
    out_block = pl.BlockSpec((1, 3, mols), lambda b: (b, 0, 0))
    arrays = [own, *others]
    specs = [block] * len(arrays)
    if base is not None:
        arrays.append(base)
        specs.append(out_block)
    pairs = count * mols * mols * len(others)
    return pl.pallas_call(
        functools.partial(pair_kernel, shifts, base is not None),
        grid=(count,),
        out_shape=jax.ShapeDtypeStruct((count, 3, mols), f32),
        in_specs=specs,
        out_specs=out_block,
        scratch_shapes=[
            VMEM((mols, 32), bf16),
            VMEM((32, mols), bf16),
            VMEM((16, mols), bf16),
            VMEM((2, PAIR_ROWS, mols), bf16),
            VMEM((16, mols), f32),
        ],
        compiler_params=pltpu.CompilerParams(vmem_limit_bytes=24 << 20),
        cost_estimate=pl.CostEstimate(flops=600 * pairs, bytes_accessed=count * mols * 64, transcendentals=0),
    )(*arrays)


def named(route, domains):
    return (lax.broadcasted_iota(jnp.int32, (domains, route.shape[1]), 0) == route).astype(f32)


def chosen(slot, capacity):
    return (lax.broadcasted_iota(jnp.int32, (capacity, slot.shape[1]), 0) == slot).astype(bf16)


def route_kernel(capacity, pos_ref, route_ref, out_ref, slot_ref, rows_s):
    mols = pos_ref.shape[-1]
    domains = out_ref.shape[0]
    mine = named(route_ref[...], domains)
    width = 128
    up_to = (
        lax.broadcasted_iota(jnp.int32, (width, width), 0) <= lax.broadcasted_iota(jnp.int32, (width, width), 1)
    ).astype(bf16)
    before = jnp.zeros((domains, 1), f32)
    slots = []
    for lo in range(0, mols, width):
        piece = mine[:, lo : lo + width]
        rank = jnp.dot(piece.astype(bf16), up_to, preferred_element_type=f32)
        slots.append(jnp.sum(piece * (rank + before - 1.0), axis=0, keepdims=True))
        before = before + jnp.sum(piece, axis=1, keepdims=True)
    slot = jnp.concatenate(slots, axis=1).astype(jnp.int32)
    slot_ref[...] = slot
    at_slot = chosen(slot, capacity)
    for part, value in enumerate(thirds(pos_ref[...])):
        for c in range(3):
            row = 3 * part + c
            rows_s[row * domains : (row + 1) * domains, :] = (mine * value[c : c + 1]).astype(bf16)
    rows_s[9 * domains :, :] = mine.astype(bf16)
    sent = lax.dot_general(rows_s[...], at_slot, (((1,), (1,)), ((), ())), preferred_element_type=f32)
    sent = sent.reshape(10, domains, capacity)
    for c in range(3):
        value = sent[c] + sent[3 + c] + sent[6 + c]
        if c == 1:
            value = value + FAR * (1.0 - sent[9])
        out_ref[:, c, :] = value
    out_ref[:, 3, :] = sent[9]


def routed(pos, route, domains, capacity):
    mols = pos.shape[-1]
    return pl.pallas_call(
        functools.partial(route_kernel, capacity),
        out_shape=(jax.ShapeDtypeStruct((domains, 4, capacity), f32), jax.ShapeDtypeStruct((1, mols), jnp.int32)),
        in_specs=[pl.BlockSpec(memory_space=VMEM)] * 2,
        out_specs=(pl.BlockSpec(memory_space=VMEM),) * 2,
        scratch_shapes=[VMEM((10 * domains, mols), bf16)],
        compiler_params=pltpu.CompilerParams(vmem_limit_bytes=24 << 20),
        cost_estimate=pl.CostEstimate(flops=1 << 30, bytes_accessed=1 << 18, transcendentals=0),
    )(pos, route)


def unroute_kernel(capacity, back_ref, route_ref, slot_ref, out_ref):
    domains = back_ref.shape[0]
    mine = named(route_ref[...], domains)
    at_slot = chosen(slot_ref[...], capacity)
    for c in range(3):
        rows = jnp.concatenate(thirds(back_ref[:, c, :]), axis=0).astype(bf16)
        spread = jnp.dot(rows, at_slot, preferred_element_type=f32)
        value = spread[:domains] + spread[domains : 2 * domains] + spread[2 * domains :]
        out_ref[c : c + 1, :] = jnp.sum(value * mine, axis=0, keepdims=True)


def unrouted(back, route, slot):
    mols = route.shape[-1]
    return pl.pallas_call(
        functools.partial(unroute_kernel, back.shape[-1]),
        out_shape=jax.ShapeDtypeStruct((3, mols), f32),
        in_specs=[pl.BlockSpec(memory_space=VMEM)] * 3,
        out_specs=pl.BlockSpec(memory_space=VMEM),
        compiler_params=pltpu.CompilerParams(vmem_limit_bytes=24 << 20),
        cost_estimate=pl.CostEstimate(flops=1 << 29, bytes_accessed=1 << 18, transcendentals=0),
    )(back, route, slot)


def body_kernel(slabs, in_ref, out_ref, pos_s, left_s, right_s, terms_s, weight_s, rho_s):
    capacity = in_ref.shape[-1]
    wide = 2 * capacity
    span = min(slabs, 2 * BAND + 2)
    mid = 0.5 * slabs
    for s in range(slabs):
        shift = jnp.where(lax.broadcasted_iota(jnp.int32, (3, 1), 0) == 0, s - mid, -0.5 * SLAB_SIDE)
        pos_s[:, s * capacity : (s + 1) * capacity] = in_ref[s, 0:3, :] + shift.astype(f32)
    pos = pos_s[...]
    left, right = factors(pos, 4.0)
    left_s[...] = left.T.astype(bf16)
    right_s[...] = right.astype(bf16)

    def start_of(tile):
        return jnp.clip(2 * tile - BAND, 0, slabs - span)

    def weigh(tile, carry):
        lanes = pl.ds(pl.multiple_of(tile * wide, wide), wide)
        at = pl.ds(pl.multiple_of(start_of(tile) * capacity, capacity), span * capacity)
        near = jnp.dot(left_s[at, :], right_s[:, lanes], preferred_element_type=f32)
        near = jnp.maximum(near, 0.0)
        weight = near * near
        rho_s[:, lanes] = jnp.sum(weight, axis=0, keepdims=True)
        weight_s[tile] = (weight * weight).astype(bf16)
        return carry

    lax.fori_loop(0, slabs // 2, weigh, 0, unroll=2)
    rho = rho_s[...]
    one = jnp.ones_like(rho)
    blank = jnp.zeros((8, pos.shape[1]), f32)
    terms_s[...] = jnp.concatenate(
        [one, *thirds(pos), *thirds(rho), *thirds(rho * pos), blank, one], axis=0
    ).astype(bf16)

    def push(tile, carry):
        lanes = pl.ds(pl.multiple_of(tile * wide, wide), wide)
        at = pl.ds(pl.multiple_of(start_of(tile) * capacity, capacity), span * capacity)
        total = jnp.dot(terms_s[:, at], weight_s[tile], preferred_element_type=f32)
        here = pos_s[:, lanes]
        plain = here * total[0:1] - (total[1:4] + total[4:7] + total[7:10])
        dense = here * (total[10:11] + total[11:12] + total[12:13]) - (total[13:16] + total[16:19] + total[19:22])
        force = f32(BODY_SCALE) * (rho_s[:, lanes] * plain + dense)
        out_ref[2 * tile, 0:3, :] = force[:, :capacity]
        out_ref[2 * tile + 1, 0:3, :] = force[:, capacity:]
        return carry

    lax.fori_loop(0, slabs // 2, push, 0, unroll=2)
    out_ref[:, 3, :] = jnp.zeros((slabs, capacity), f32)


def body_forces(inbox):
    slabs, _, capacity = inbox.shape
    total = slabs * capacity
    span = min(slabs, 2 * BAND + 2)
    return pl.pallas_call(
        functools.partial(body_kernel, slabs),
        out_shape=jax.ShapeDtypeStruct((slabs, 4, capacity), f32),
        in_specs=[pl.BlockSpec(memory_space=VMEM)],
        out_specs=pl.BlockSpec(memory_space=VMEM),
        scratch_shapes=[
            VMEM((3, total), f32),
            VMEM((total, 32), bf16),
            VMEM((32, total), bf16),
            VMEM((31, total), bf16),
            VMEM((slabs // 2, span * capacity, 2 * capacity), bf16),
            VMEM((1, total), f32),
        ],
        compiler_params=pltpu.CompilerParams(vmem_limit_bytes=32 << 20),
        cost_estimate=pl.CostEstimate(flops=1 << 32, bytes_accessed=1 << 18, transcendentals=0),
    )(inbox)


def shards(centroid, bead_offsets, routes):
    beads_dev, _, mols = bead_offsets.shape
    domains = lax.axis_size("space")
    capacity = 2 * mols // domains
    scale = np.array([1.0, SLAB_SIDE, SLAB_SIDE], np.float32)
    q = scale[None, :, None] * centroid[None] + bead_offsets
    nxt = passed_along(q, "space", -1)
    prev = passed_along(q, "space", 1)

    table = jnp.asarray(contract_table())
    first = lax.axis_index("bead") * beads_dev
    local = lax.dynamic_slice_in_dim(table, first, beads_dev, 1)
    partial = jnp.einsum("kb,bcm->kcm", local, q, precision=lax.Precision.HIGHEST)
    arrived = lax.all_to_all(partial, "bead", split_axis=0, concat_axis=0, tiled=True)
    coarse = arrived.sum(axis=0)
    route = routes.reshape(1, mols)
    outbox, slot = routed(coarse, route, domains, capacity)
    inbox = lax.all_to_all(outbox, "space", split_axis=0, concat_axis=0, tiled=True)
    back = lax.all_to_all(body_forces(inbox), "space", split_axis=0, concat_axis=0, tiled=True)
    mine = unrouted(back, route, slot)
    copies = jnp.broadcast_to(mine, (CONTRACTED, *mine.shape))
    every = lax.all_to_all(copies, "bead", split_axis=0, concat_axis=0, tiled=True)

    own = pair_forces(q, [q], (0.0,), None, 0, beads_dev)
    pair2 = pair_forces(q, [prev, nxt], (-1.0, 1.0), own, 0, beads_dev)
    expand = local.T * (BEADS / CONTRACTED)
    spread = jnp.einsum("bk,kcm->bcm", expand, every, precision=lax.Precision.HIGHEST)
    return pair2 + spread


def solution(mesh):
    placed = (P(None, "space"), P("bead", None, "space"), P("space", None))
    return jax.shard_map(
        shards, mesh=mesh, in_specs=placed, out_specs=P("bead", None, "space"), check_vma=False
    )
```

time: 538 us -> 156 us (0.29)
  other arithmetic: 422 us -> 2.11 us
  Pallas kernels: 0 us -> 112 us
  local copies, waits for them, and re-layouts: 54.8 us -> 3.54 us
  waiting for transfers between devices: 20.7 us -> 1.46 us
  blocking collectives: 0 us -> 8.04 us
  starting transfers between devices: 32.9 us -> 27.1 us
    reduce_sum x162 -> x1, other arithmetic: 321 us -> 0.03 us  [shards(): coarse = arrived.sum(axis=0)]
    pallas_call x0 -> x5, Pallas kernels: none -> 112 us  [the longest x2 102 us: pair_forces(): pl.pallas_call(functools.partial(pair_kernel, shifts, base is not None),...]
    mul x75 -> x1, other arithmetic: 83.9 us -> 0.83 us  [shards(): q = scale[None, :, None] * centroid[None] + bead_offsets]
    dynamic_update_slice x112 -> x0, local copies, waits for them, and re-layouts: 28.7 us -> none  [the longest x32 27.4 us: shards(): partial_pair, reaction = lax.map(one_bead, (q, nearby))]
    gather x2 -> x0, local copies, waits for them, and re-layouts: 13.4 us -> none  [shards(): mine = returned[:, :, route, slot]]
    ppermute x2, waiting for transfers between devices: 10.5 us -> 0.01 us  [passed_along(): lax.ppermute(value, axis, [(i, (i + by) % peers) for i in range(peers)])]
    another operation x7 -> x0, other arithmetic: 9.41 us -> none
    all_to_all x4 -> x3, waiting for transfers between devices: 10.3 us -> 1.46 us  [the longest x1 1.45 us: shards(): lax.all_to_all(outbox, 'space', split_axis=0, concat_axis=0, tiled=True)]
  transfers between devices with their start and end apart: 6 -> 5, of which waited for: 3 -> 1; matrix products, arithmetic and copies ran while one was open for 87% -> 0% of each run, Pallas kernels for 0% -> 71%
where the time goes in v1:
time: 156 us; the launch traced here: 155 us
  Pallas kernels  112 us (72%)
  starting transfers between devices  27.1 us (17%)
  blocking collectives  8.04 us (5%)
  local copies, waits for them, and re-layouts  3.54 us (2%)
  other arithmetic  2.11 us (1%)
    pallas_call x2, Pallas kernels, pair_forces(): pl.pallas_call(functools.partial(pair_kernel, shifts, base is not None),...  102 us
    all_to_all x1, starting transfers between devices, shards(): lax.all_to_all(outbox, 'space', split_axis=0, concat_axis=0, tiled=True)  10.1 us
    pallas_call x1, Pallas kernels, body_forces(): pl.pallas_call(functools.partial(body_kernel, slabs), out_shape=jax.Shape...  8.38 us
    all_to_all x1, blocking collectives, shards(): lax.all_to_all(partial, 'bead', split_axis=0, concat_axis=0, tiled=True)  8.04 us
    ppermute x2, starting transfers between devices, passed_along(): lax.ppermute(value, axis, [(i, (i + by) % peers) for i in range(peers)])  7.26 us
    all_to_all x1, starting transfers between devices, shards(): lax.all_to_all(copies, 'bead', split_axis=0, concat_axis=0, tiled=True)  5.97 us
    all_to_all x1, starting transfers between devices, shards(): lax.all_to_all(body_forces(inbox), 'space', split_axis=0, concat_axis=0,...  3.85 us
  transfers between devices with their start and end apart: 5, of which 1 were waited for; matrix products, arithmetic and copies ran while one was open for 0% of the time, Pallas kernels for 71%

profile of v1, /device:TPU:1, one launch (start us, length us, event | category | flops | bytes accessed | tf_op | source)
XLA Modules:
  0.0 155.1 jit_solution(14638029889708754262)
XLA Ops:
  0.0 0.0 copy-start.2
  0.0 0.7 copy-done.2
  0.7 0.8 broadcast_multiply_fusion
  1.5 1.1 copy_add_fusion.1.refs_0_.refs_1_
  2.6 0.0 copy-start.1
  2.6 0.7 copy-done.1
  3.2 0.4 fusion
  3.6 0.1 copy.18
  3.7 8.0 %all_to_all.20 = f32[4,3,2048]{2,1,0:T(4,128)S(1)} all-to-all(f32[4,3,2048]{2,1,0:T(4,128)S(1)} %copy.18), channel_id=1, replica_groups=mesh['bead'=4,'space'=32] {'bead'}, dimensions={0} | all-to-all | bytes 196608 | tf_op jit(solution)/shard_map/all_to_all | solution.py:303
  11.8 0.0 copy-start
  11.8 0.7 copy-done
  12.5 1.4 shard_map.57
  13.8 10.1 %all-to-all-start.1 = ((f32[32,4,128]{2,1,0:T(4,128)}), f32[32,4,128]{2,1,0:T(4,128)S(1)}, u32[]{:S(2)}, u32[]{:S(2)}) async-start(f32[32,4,128]{2,1,0:T(4,128)} %get-tuple-element.7), calls=%async_computation.1 | async-start | bytes 131072 | tf_op jit(solution)/shard_map/all_to_all | solution.py:307
  23.9 1.3 collective-permute-start
  25.2 6.0 %collective-permute-start.1 = (f32[8,3,2048]{2,1,0:T(4,128)S(1)}, f32[8,3,2048]{2,1,0:T(4,128)S(1)}, u32[]{:S(2)}, u32[]{:S(2)}) collective-permute-start(f32[8,3,2048]{2,1,0:T(4,128)S(1)} %copy_add_fusion.1.refs_0_.refs_1_), channel_id=1, source_target_pairs={{0,31},{1,0},{2,1},{3,2},{4,3},{5,4},{6,5},{7,6},{8,7},{9,8},{10,9... | collective-permute-start | bytes 589832 | tf_op jit(solution)/shard_map/ppermute | solution.py:31
  31.2 1.5 all-to-all-done.1.in_ref
  32.6 8.4 %shard_map.58 = f32[32,4,128]{2,1,0:T(4,128)} custom-call(f32[32,4,128]{2,1,0:T(4,128)S(1)} %all-to-all-done.1.in_ref), custom_call_target="tpu_custom_call" | custom-call | flops 4294967296 | bytes 262144 | tf_op jit(solution)/shard_map/pallas_call | solution.py:272
  41.0 3.9 %all-to-all-start.2 = ((f32[32,4,128]{2,1,0:T(4,128)}), f32[32,4,128]{2,1,0:T(4,128)S(1)}, u32[]{:S(2)}, u32[]{:S(2)}) async-start(f32[32,4,128]{2,1,0:T(4,128)} %shard_map.58), calls=%async_computation.2 | async-start | bytes 131072 | tf_op jit(solution)/shard_map/all_to_all | solution.py:308
  44.8 34.0 %shard_map.55.refs_3_ = f32[8,3,2048]{2,1,0:T(4,128)S(1)} custom-call(f32[8,3,2048]{2,1,0:T(4,128)S(1)} %copy_add_fusion.1.refs_0_.refs_1_, f32[8,3,2048]{2,1,0:T(4,128)S(1)} %copy_add_fusion.1.refs_0_.refs_1_), custom_call_target="tpu_custom_call" | custom-call | flops 20132659200 | bytes 1048576 | tf_op jit(solution)/shard_map/pallas_call | solution.py:123
  78.9 0.0 all-to-all-done.2.back_ref
  78.9 0.6 shard_map.59
  79.5 0.7 broadcast_in_dim.4
  80.1 6.0 %all-to-all-start.3 = ((f32[4,3,2048]{2,1,0:T(4,128)}), f32[4,3,2048]{2,1,0:T(4,128)S(1)}, u32[]{:S(2)}, u32[]{:S(2)}) async-start(f32[4,3,2048]{2,1,0:T(4,128)} %broadcast_in_dim.4), calls=%async_computation.3 | async-start | bytes 262144 | tf_op jit(solution)/shard_map/all_to_all | solution.py:311
  86.1 0.0 collective-permute-done.refs_1_
  86.1 0.0 collective-permute-done.1.refs_2_
  86.1 67.5 %shard_map.56 = f32[8,3,2048]{2,1,0:T(4,128)S(1)} custom-call(f32[8,3,2048]{2,1,0:T(4,128)S(1)} %copy_add_fusion.1.refs_0_.refs_1_, f32[8,3,2048]{2,1,0:T(4,128)S(1)} %collective-permute-done.refs_1_, f32[8,3,2048]{2,1,0:T(4,128)S(1)} %collective-permute-done.1.refs_2_, f32[8,3,2048]{2,1,0:T(4,128)S(1)} %shard_map.55.refs_3_), custom_call_target="tpu_custom_call" | custom-call | flops 40265318400 | bytes 1048576 | tf_op jit(solution)/shard_map/pallas_call | solution.py:123
  153.7 0.0 all-to-all-done.3
  153.7 0.4 fusion.2
  154.1 0.2 copy_add_fusion
  154.3 0.8 copy.21
  (1 shorter events, 0.0 us)
Async XLA Ops:
  0.0 0.7 copy-start.2
  2.6 0.7 copy-start.1
  11.8 0.7 copy-start
  13.8 18.8 %all-to-all-start.1 = ((f32[32,4,128]{2,1,0:T(4,128)}), f32[32,4,128]{2,1,0:T(4,128)S(1)}, u32[]{:S(2)}, u32[]{:S(2)}) async-start(f32[32,4,128]{2,1,0:T(4,128)} %get-tuple-element.7), calls=%async_computation.1 | async-start | bytes 131072 | tf_op jit(solution)/shard_map/all_to_all | solution.py:307
  23.9 62.2 %collective-permute-start = (f32[8,3,2048]{2,1,0:T(4,128)S(1)}, f32[8,3,2048]{2,1,0:T(4,128)S(1)}, u32[]{:S(2)}, u32[]{:S(2)}) collective-permute-start(f32[8,3,2048]{2,1,0:T(4,128)S(1)} %copy_add_fusion.1.refs_0_.refs_1_), channel_id=1, source_target_pairs={{0,1},{1,2},{2,3},{3,4},{4,5},{5,6},{6,7},{7,8},{8,9},{9,10},{10,1... | collective-permute-start | bytes 589832 | tf_op jit(solution)/shard_map/ppermute | solution.py:31
  25.2 60.9 %collective-permute-start.1 = (f32[8,3,2048]{2,1,0:T(4,128)S(1)}, f32[8,3,2048]{2,1,0:T(4,128)S(1)}, u32[]{:S(2)}, u32[]{:S(2)}) collective-permute-start(f32[8,3,2048]{2,1,0:T(4,128)S(1)} %copy_add_fusion.1.refs_0_.refs_1_), channel_id=1, source_target_pairs={{0,31},{1,0},{2,1},{3,2},{4,3},{5,4},{6,5},{7,6},{8,7},{9,8},{10,9... | collective-permute-start | bytes 589832 | tf_op jit(solution)/shard_map/ppermute | solution.py:31
  41.0 37.9 %all-to-all-start.2 = ((f32[32,4,128]{2,1,0:T(4,128)}), f32[32,4,128]{2,1,0:T(4,128)S(1)}, u32[]{:S(2)}, u32[]{:S(2)}) async-start(f32[32,4,128]{2,1,0:T(4,128)} %shard_map.58), calls=%async_computation.2 | async-start | bytes 131072 | tf_op jit(solution)/shard_map/all_to_all | solution.py:308
  80.1 73.5 %all-to-all-start.3 = ((f32[4,3,2048]{2,1,0:T(4,128)}), f32[4,3,2048]{2,1,0:T(4,128)S(1)}, u32[]{:S(2)}, u32[]{:S(2)}) async-start(f32[4,3,2048]{2,1,0:T(4,128)} %broadcast_in_dim.4), calls=%async_computation.3 | async-start | bytes 262144 | tf_op jit(solution)/shard_map/all_to_all | solution.py:311
